TPU v7x, 32 devices: a whole 2x2x4 slice. The times are simulated.
32 devices in a mesh: sx: 8 (over y, x, core), sy: 4 (over z).
Axes of the slice: x: 2, y: 2, z: 4, core: 2. Of those that a mesh axis runs over, the one named last changes fastest.
Arguments:
- adjoint_loads: float32 [8, 8, 2, 288, 128], P('sx', 'sy'), may hold values from -6 to 6
- dual_taut: bfloat16 [8, 8, 1152, 1152], P('sx', 'sy'), may hold values from -1 to 2
- dual_wrinkle: bfloat16 [8, 8, 1152, 1152], P('sx', 'sy'), may hold values from -1 to 2
- dirichlet_taut: bfloat16 [8, 8, 1152, 1152], P('sx', 'sy'), may hold values from -1 to 2
- dirichlet_wrinkle: bfloat16 [8, 8, 1152, 1152], P('sx', 'sy'), may hold values from -1 to 2
- coupling: bfloat16 [8, 8, 12, 1152], P('sx', 'sy'), may hold values from -0.25 to 0.25
- coarse_inverse: bfloat16 [256, 256], P('sx', 'sy'), may hold values from -1 to 2
- wrinkled: int32 [8, 8], P('sx', 'sy'), may hold values 0 or 1
- edge_lengths: int32 [8, 8, 2], P('sx', 'sy'), may hold values from 144 to 288
- corner_map: int32 [8, 8, 12], P('sx', 'sy'), may hold values from 0 to 255, as said below
Outputs:
- multipliers: float32 [8, 8, 2, 288, 128], P('sx', 'sy')
- preconditioned: float32 [8, 8, 2, 288, 128], P('sx', 'sy')
Inputs may be any that keep to these rules, and one draw needn't show every extreme that they name: `corner_map`: each subdomain names 12 distinct coarse indices, three for each of its four grid corners; subdomains that meet at a grid corner name the same three indices for it; distinct grid corners name distinct indices.
All inputs are finite; a program needn't handle non-finite values. No bound on the sum of `wrinkled` on one device may be relied on, other than what follows from the above.
Results may differ from a plain program's by a relative error of at most 0.012.
Values may be sent and summed in bfloat16 or wider, within the bound.
A program may use at most 64 MiB of HBM per device.

v0:
```python
import jax
import jax.numpy as jnp
from jax import lax
from jax.sharding import PartitionSpec as P

EDGE = 288
CORNERS = 12
ITERS = 2


step_sizes = (0.55, 0.75)
momenta = (0.0, 0.15)


def from_behind(shard, axis, by):
    peers = lax.axis_size(axis)
    pairs = [(i, i + by) for i in range(peers) if 0 <= i + by < peers]
    return lax.ppermute(shard, axis, pairs)


def edge_mask(edge_lengths):
    per_row = edge_lengths.shape[1]
    shape_all = (1, per_row, 2, EDGE)
    positions = lax.broadcasted_iota(jnp.int32, shape_all, 3)
    inside = positions < edge_lengths[:, :, :, None]
    columns = lax.axis_index("sy") * per_row + lax.broadcasted_iota(jnp.int32, shape_all, 1)
    edge_kind = lax.broadcasted_iota(jnp.int32, shape_all, 2)
    exists = jnp.where(
        edge_kind == 0,
        columns < per_row * lax.axis_size("sy") - 1,
        lax.axis_index("sx") < lax.axis_size("sx") - 1,
    )
    return (inside & exists).astype(jnp.float32)[..., None]


def spread(edges):
    east_edge = edges[:, :, 0]
    south_edge = edges[:, :, 1]
    from_left = from_behind(east_edge[:, -1:], "sy", 1)
    west_edge = jnp.concatenate([from_left, east_edge[:, :-1]], axis=1)
    north_edge = from_behind(south_edge, "sx", 1)
    return jnp.concatenate([east_edge, south_edge, -west_edge, -north_edge], axis=2)


def collect(local_part):
    west_part = local_part[:, :, 2 * EDGE : 3 * EDGE]
    from_right = from_behind(west_part[:, :1], "sy", -1)
    right_west = jnp.concatenate([west_part[:, 1:], from_right], axis=1)
    down_north = from_behind(local_part[:, :, 3 * EDGE :], "sx", -1)
    return jnp.stack(
        [local_part[:, :, :EDGE] - right_west, local_part[:, :, EDGE : 2 * EDGE] - down_north],
        axis=2,
    )


def paired(taut, wrinkle, wrinkled, vectors):
    base_part = jnp.einsum("rsij,rsjl->rsil", taut, vectors, preferred_element_type=jnp.float32)
    extra_part = jnp.einsum("rsij,rsjl->rsil", wrinkle, vectors, preferred_element_type=jnp.float32)
    return base_part + wrinkled.astype(jnp.float32)[:, :, None, None] * extra_part


def coarse_term(coupling, corner_map, coarse_inverse, vectors):
    col_count = coarse_inverse.shape[1]
    coarse_order = col_count * lax.axis_size("sy")
    corner_terms = jnp.einsum(
        "rskj,rsjl->rskl", coupling, vectors, preferred_element_type=jnp.float32
    )
    corner_terms = corner_terms.reshape(-1, corner_terms.shape[-1])
    corner_index = corner_map.reshape(-1)
    selector = corner_index[:, None] == lax.broadcasted_iota(
        jnp.int32, (corner_index.shape[0], coarse_order), 1
    )
    selector_float = selector.astype(jnp.float32)
    placed = jnp.einsum("kc,kl->cl", selector_float, corner_terms, precision=lax.Precision.HIGHEST)
    totals = lax.psum(placed, ("sx", "sy"))
    column_part = lax.dynamic_slice_in_dim(totals, lax.axis_index("sy") * col_count, col_count, 0)
    row_part = jnp.dot(
        coarse_inverse, column_part.astype(jnp.bfloat16), preferred_element_type=jnp.float32
    )
    solved = lax.psum(row_part, "sy").astype(jnp.bfloat16)
    selector_half = selector.astype(jnp.bfloat16)
    selected = jnp.dot(
        selector_half,
        lax.all_gather(solved, "sx", axis=0, tiled=True),
        preferred_element_type=jnp.float32,
    )
    selected = selected.astype(jnp.bfloat16).reshape(
        vectors.shape[0], vectors.shape[1], CORNERS, -1
    )
    return jnp.einsum("rskj,rskl->rsjl", coupling, selected, preferred_element_type=jnp.float32)


def local(
    adjoint_loads,
    dual_taut,
    dual_wrinkle,
    dirichlet_taut,
    dirichlet_wrinkle,
    coupling,
    coarse_inverse,
    wrinkled,
    edge_lengths,
    corner_map,
):
    masking = edge_mask(edge_lengths)
    loads = adjoint_loads * masking

    def precondition(incoming):
        vectors = spread((0.5 * incoming).astype(jnp.bfloat16))
        return 0.5 * collect(paired(dirichlet_taut, dirichlet_wrinkle, wrinkled, vectors)) * masking

    multipliers = jnp.zeros_like(loads)
    direction = jnp.zeros_like(loads)
    residual = loads
    for number in range(ITERS):
        direction = precondition(residual) + momenta[number] * direction
        multipliers = multipliers + step_sizes[number] * direction
        dual_vectors = spread(multipliers.astype(jnp.bfloat16))
        local_part = paired(dual_taut, dual_wrinkle, wrinkled, dual_vectors)
        local_part = local_part + coarse_term(coupling, corner_map, coarse_inverse, dual_vectors)
        residual = loads - collect(local_part) * masking
    return (multipliers, precondition(residual))


def solution(mesh):
    placed = (
        P("sx", "sy", None, None, None),
        P("sx", "sy", None, None),
        P("sx", "sy", None, None),
        P("sx", "sy", None, None),
        P("sx", "sy", None, None),
        P("sx", "sy", None, None),
        P("sx", "sy"),
        P("sx", "sy"),
        P("sx", "sy", None),
        P("sx", "sy", None),
    )
    return jax.shard_map(
        local,
        mesh=mesh,
        in_specs=placed,
        out_specs=(P("sx", "sy", None, None, None), P("sx", "sy", None, None, None)),
        check_vma=False,
    )
```

profile of v0, /device:TPU:1, one launch (start us, length us, event | category | flops | bytes accessed | tf_op | source)
XLA Modules:
  0.0 320.2 jit_solution(4290553914124060883)
XLA Ops:
  3.0 4.0 %collective-permute-start = (bf16[1,1,288,128]{2,3,1,0:T(8,128)(2,1)S(1)}, bf16[1,1,288,128]{2,3,1,0:T(8,128)(2,1)S(1)}, u32[]{:S(2)}, u32[]{:S(2)}) collective-permute-start(bf16[1,1,288,128]{2,3,1,0:T(8,128)(2,1)S(1)} %get-tuple-element.48), channel_id=1, source_target_pairs={{0,1},{1,2},{2,3},{4,5},{5,6},{6,7},{8,9},{9,10},{10,11},{12,13},{... | collective-permute-start | bytes 221192 | tf_op jit(solution)/shard_map/ppermute | solution.py:18
  7.0 4.0 %collective-permute-start.1 = (bf16[1,2,288,128]{2,3,1,0:T(8,128)(2,1)S(1)}, bf16[1,2,288,128]{2,3,1,0:T(8,128)(2,1)S(1)}, u32[]{:S(2)}, u32[]{:S(2)}) collective-permute-start(bf16[1,2,288,128]{2,3,1,0:T(8,128)(2,1)S(1)} %get-tuple-element.38), channel_id=1, source_target_pairs={{0,4},{4,8},{8,12},{12,16},{16,20},{20,24},{24,28},{1,5},{5,9},{9,... | collective-permute-start | bytes 442376 | tf_op jit(solution)/shard_map/ppermute | solution.py:18
  14.2 4.3 %fusion.29 = f32[2,128,1152]{2,1,0:T(8,128)S(1)} fusion(bf16[1,2,1152,1152]{3,2,1,0:T(8,128)(2,1)} %param.14, bf16[1,2,1152,128]{2,3,1,0:T(8,128)(2,1)S(1)} %concatenate.138, f32[2]{0:T(128)S(1)} %convert_bitcast_fusion), kind=kOutput, calls=%fused_computation.23 | convolution fusion | flops 679772160 | bytes 7077896 | tf_op jit(solution)/shard_map/rsij,rsjl->rsil/dot_general | solution.py:58
  21.8 5.1 %collective-permute-done.2 = f32[1,1,288,128]{2,3,1,0:T(8,128)S(1)} collective-permute-done((f32[1,1,288,128]{2,3,1,0:T(8,128)S(1)}, f32[1,1,288,128]{2,3,1,0:T(8,128)S(1)}, u32[]{:S(2)}, u32[]{:S(2)}) %collective-permute-start.2) | collective-permute-done | bytes 147488 | tf_op jit(solution)/shard_map/ppermute | solution.py:18
  29.1 9.2 %collective-permute-done.3 = f32[1,2,288,128]{2,3,1,0:T(8,128)S(1)} collective-permute-done((f32[1,2,288,128]{2,3,1,0:T(8,128)S(1)}, f32[1,2,288,128]{2,3,1,0:T(8,128)S(1)}, u32[]{:S(2)}, u32[]{:S(2)}) %collective-permute-start.3) | collective-permute-done | bytes 294944 | tf_op jit(solution)/shard_map/ppermute | solution.py:18
  39.3 3.2 collective-permute-start.4
  50.0 41.2 %all-reduce.2 = bf16[256,128]{1,0:T(8,128)(2,1)S(1)} all-reduce(f32[256,128]{1,0:T(8,128)S(1)} %fusion.109), channel_id=1, replica_groups=mesh['sx'=8,'sy'=4] {'sx','sy'}, use_global_device_ids=true, to_apply=%region_0.1 | all-reduce | flops 32768 | bytes 196608 | tf_op jit(solution)/shard_map/psum | solution.py:75
  92.1 13.2 %psum.29 = bf16[32,128]{1,0:T(8,128)(2,1)S(1)} all-reduce(f32[32,128]{1,0:T(8,128)S(1)} %convolution_bitcast_fusion.1), channel_id=1, replica_groups=mesh['sx'=8,'sy'=4] {'sy'}, use_global_device_ids=true, to_apply=%region_1.2 | all-reduce | flops 4096 | bytes 24576 | tf_op jit(solution)/shard_map/psum | solution.py:80
  105.2 15.1 %all_gather.6 = bf16[256,128]{1,0:T(8,128)(2,1)S(1)} all-gather(bf16[32,128]{1,0:T(8,128)(2,1)S(1)} %psum.29), channel_id=1, replica_groups=mesh['sx'=8,'sy'=4] {'sx'}, dimensions={0}, use_global_device_ids=true | all-gather | bytes 73728 | tf_op jit(solution)/shard_map/all_gather | solution.py:84
  120.9 4.4 %fusion.44 = f32[2,128,1152]{2,1,0:T(8,128)S(1)} fusion(bf16[1,2,1152,1152]{3,2,1,0:T(8,128)(2,1)} %param.12, bf16[1,2,1152,128]{2,3,1,0:T(8,128)(2,1)S(1)} %concatenate.141, f32[2]{0:T(128)S(1)} %convert_bitcast_fusion), kind=kOutput, calls=%fused_computation.28 | convolution fusion | flops 679772160 | bytes 7077896 | tf_op jit(solution)/shard_map/rsij,rsjl->rsil/dot_general | solution.py:58
  128.5 6.9 %collective-permute-done.6 = f32[1,1,288,128]{2,3,1,0:T(8,128)S(1)} collective-permute-done((f32[1,1,288,128]{2,3,1,0:T(8,128)S(1)}, f32[1,1,288,128]{2,3,1,0:T(8,128)S(1)}, u32[]{:S(2)}, u32[]{:S(2)}) %collective-permute-start.6) | collective-permute-done | bytes 147488 | tf_op jit(solution)/shard_map/ppermute | solution.py:18
  135.6 2.9 collective-permute-start.7
  138.5 7.0 %collective-permute-done.7 = f32[1,2,288,128]{2,3,1,0:T(8,128)S(1)} collective-permute-done((f32[1,2,288,128]{2,3,1,0:T(8,128)S(1)}, f32[1,2,288,128]{2,3,1,0:T(8,128)S(1)}, u32[]{:S(2)}, u32[]{:S(2)}) %collective-permute-start.7) | collective-permute-done | bytes 294944 | tf_op jit(solution)/shard_map/ppermute | solution.py:18
  149.4 2.5 collective-permute-done.9
  152.5 4.2 %fusion.32 = f32[2,128,1152]{2,1,0:T(8,128)S(1)} fusion(bf16[1,2,1152,1152]{3,2,1,0:T(8,128)(2,1)} %param.14, bf16[1,2,1152,128]{2,3,1,0:T(8,128)(2,1)S(1)} %concatenate.144, f32[2]{0:T(128)S(1)} %convert_bitcast_fusion), kind=kOutput, calls=%fused_computation.24 | convolution fusion | flops 679772160 | bytes 7077896 | tf_op jit(solution)/shard_map/rsij,rsjl->rsil/dot_general | solution.py:58
  156.7 4.2 %fusion.65 = f32[1,2,1152,128]{2,3,1,0:T(8,128)S(1)} fusion(f32[2,128,1152]{2,1,0:T(8,128)S(1)} %fusion.32, bf16[1,2,1152,1152]{3,2,1,0:T(8,128)(2,1)} %param.13, bf16[1,2,1152,128]{2,3,1,0:T(8,128)(2,1)S(1)} %concatenate.144), kind=kOutput, calls=%fused_computation.35 | convolution fusion | flops 679772160 | bytes 8257536 | tf_op jit(solution)/shard_map/rsij,rsjl->rsil/dot_general | solution.py:57
  162.4 6.6 %collective-permute-done.10 = f32[1,1,288,128]{2,3,1,0:T(8,128)S(1)} collective-permute-done((f32[1,1,288,128]{2,3,1,0:T(8,128)S(1)}, f32[1,1,288,128]{2,3,1,0:T(8,128)S(1)}, u32[]{:S(2)}, u32[]{:S(2)}) %collective-permute-start.10) | collective-permute-done | bytes 147488 | tf_op jit(solution)/shard_map/ppermute | solution.py:18
  171.3 8.1 %collective-permute-done.11 = f32[1,2,288,128]{2,3,1,0:T(8,128)S(1)} collective-permute-done((f32[1,2,288,128]{2,3,1,0:T(8,128)S(1)}, f32[1,2,288,128]{2,3,1,0:T(8,128)S(1)}, u32[]{:S(2)}, u32[]{:S(2)}) %collective-permute-start.11) | collective-permute-done | bytes 294944 | tf_op jit(solution)/shard_map/ppermute | solution.py:18
  180.8 2.5 collective-permute-start.12
  185.4 2.5 collective-permute-done.13
  188.8 4.2 %fusion.47 = f32[2,128,1152]{2,1,0:T(8,128)S(1)} fusion(bf16[1,2,1152,1152]{3,2,1,0:T(8,128)(2,1)} %param.12, bf16[1,2,1152,128]{2,3,1,0:T(8,128)(2,1)S(1)} %concatenate.147, f32[2]{0:T(128)S(1)} %convert_bitcast_fusion), kind=kOutput, calls=%fused_computation.29 | convolution fusion | flops 679772160 | bytes 7077896 | tf_op jit(solution)/shard_map/rsij,rsjl->rsil/dot_general | solution.py:58
  193.4 39.6 %all-reduce.3 = bf16[256,128]{1,0:T(8,128)(2,1)S(1)} all-reduce(f32[256,128]{1,0:T(8,128)S(1)} %fusion.108), channel_id=1, replica_groups=mesh['sx'=8,'sy'=4] {'sx','sy'}, use_global_device_ids=true, to_apply=%region_2.3 | all-reduce | flops 32768 | bytes 196608 | tf_op jit(solution)/shard_map/psum | solution.py:75
  233.2 13.5 %psum.31 = bf16[32,128]{1,0:T(8,128)(2,1)S(1)} all-reduce(f32[32,128]{1,0:T(8,128)S(1)} %convolution_bitcast_fusion), channel_id=1, replica_groups=mesh['sx'=8,'sy'=4] {'sy'}, use_global_device_ids=true, to_apply=%region_3.4 | all-reduce | flops 4096 | bytes 24576 | tf_op jit(solution)/shard_map/psum | solution.py:80
  246.7 15.0 %all_gather.7 = bf16[256,128]{1,0:T(8,128)(2,1)S(1)} all-gather(bf16[32,128]{1,0:T(8,128)(2,1)S(1)} %psum.31), channel_id=1, replica_groups=mesh['sx'=8,'sy'=4] {'sx'}, dimensions={0}, use_global_device_ids=true | all-gather | bytes 73728 | tf_op jit(solution)/shard_map/all_gather | solution.py:84
  262.3 4.2 %fusion.59 = f32[1,2,1152,128]{2,3,1,0:T(8,128)S(1)} fusion(f32[2,128,1152]{2,1,0:T(8,128)S(1)} %fusion.102, f32[2,128,1152]{2,1,0:T(8,128)S(1)} %fusion.47, bf16[1,2,1152,1152]{3,2,1,0:T(8,128)(2,1)} %param.11, bf16[1,2,1152,128]{2,3,1,0:T(8,128)(2,1)S(1)} %concatenate.147), kind=kOutput, calls=%fused_computation.33 | convolution fusion | flops 680067072 | bytes 9437184 | tf_op jit(solution)/shard_map/rsij,rsjl->rsil/dot_general | solution.py:57
  268.0 6.9 %collective-permute-done.14 = f32[1,1,288,128]{2,3,1,0:T(8,128)S(1)} collective-permute-done((f32[1,1,288,128]{2,3,1,0:T(8,128)S(1)}, f32[1,1,288,128]{2,3,1,0:T(8,128)S(1)}, u32[]{:S(2)}, u32[]{:S(2)}) %collective-permute-start.14) | collective-permute-done | bytes 147488 | tf_op jit(solution)/shard_map/ppermute | solution.py:18
  275.0 2.9 collective-permute-start.15
  278.0 7.0 %collective-permute-done.15 = f32[1,2,288,128]{2,3,1,0:T(8,128)S(1)} collective-permute-done((f32[1,2,288,128]{2,3,1,0:T(8,128)S(1)}, f32[1,2,288,128]{2,3,1,0:T(8,128)S(1)}, u32[]{:S(2)}, u32[]{:S(2)}) %collective-permute-start.15) | collective-permute-done | bytes 294944 | tf_op jit(solution)/shard_map/ppermute | solution.py:18
  292.0 4.2 %fusion.35 = f32[2,128,1152]{2,1,0:T(8,128)S(1)} fusion(bf16[1,2,1152,1152]{3,2,1,0:T(8,128)(2,1)} %param.14, bf16[1,2,1152,128]{2,3,1,0:T(8,128)(2,1)S(1)} %concatenate.150, f32[2]{0:T(128)S(1)} %convert_bitcast_fusion), kind=kOutput, calls=%fused_computation.25 | convolution fusion | flops 679772160 | bytes 7077896 | tf_op jit(solution)/shard_map/rsij,rsjl->rsil/dot_general | solution.py:58
  296.2 4.2 %fusion.62 = f32[1,2,1152,128]{2,3,1,0:T(8,128)S(1)} fusion(f32[2,128,1152]{2,1,0:T(8,128)S(1)} %fusion.35, bf16[1,2,1152,1152]{3,2,1,0:T(8,128)(2,1)} %param.13, bf16[1,2,1152,128]{2,3,1,0:T(8,128)(2,1)S(1)} %concatenate.150), kind=kOutput, calls=%fused_computation.34 | convolution fusion | flops 679772160 | bytes 8257536 | tf_op jit(solution)/shard_map/rsij,rsjl->rsil/dot_general | solution.py:57
  302.0 6.6 %collective-permute-done.18 = f32[1,1,288,128]{2,3,1,0:T(8,128)S(1)} collective-permute-done((f32[1,1,288,128]{2,3,1,0:T(8,128)S(1)}, f32[1,1,288,128]{2,3,1,0:T(8,128)S(1)}, u32[]{:S(2)}, u32[]{:S(2)}) %collective-permute-start.18) | collective-permute-done | bytes 147488 | tf_op jit(solution)/shard_map/ppermute | solution.py:18
  311.9 7.0 %collective-permute-done.19 = f32[1,2,288,128]{2,3,1,0:T(8,128)S(1)} collective-permute-done((f32[1,2,288,128]{2,3,1,0:T(8,128)S(1)}, f32[1,2,288,128]{2,3,1,0:T(8,128)S(1)}, u32[]{:S(2)}, u32[]{:S(2)}) %collective-permute-start.19) | collective-permute-done | bytes 294944 | tf_op jit(solution)/shard_map/ppermute | solution.py:18
  (110 shorter events, 52.1 us)
Async XLA Ops:
  0.6 48.7 %copy-start = (bf16[1,2,12,1152]{3,1,2,0:T(2,128)(2,1)S(1)}, bf16[1,2,12,1152]{3,1,2,0:T(2,128)(2,1)}, u32[]{:S(2)}) copy-start(bf16[1,2,12,1152]{3,1,2,0:T(2,128)(2,1)} %param.15) | copy-start | bytes 165892
  2.8 8.2 %copy-start.5 = (s32[1,2]{1,0:T(1,128)S(1)}, s32[1,2]{1,0:T(1,128)}, u32[]{:S(2)}) copy-start(s32[1,2]{1,0:T(1,128)} %param.17) | copy-start | bytes 28
  3.0 8.0 %collective-permute-start = (bf16[1,1,288,128]{2,3,1,0:T(8,128)(2,1)S(1)}, bf16[1,1,288,128]{2,3,1,0:T(8,128)(2,1)S(1)}, u32[]{:S(2)}, u32[]{:S(2)}) collective-permute-start(bf16[1,1,288,128]{2,3,1,0:T(8,128)(2,1)S(1)} %get-tuple-element.48), channel_id=1, source_target_pairs={{0,1},{1,2},{2,3},{4,5},{5,6},{6,7},{8,9},{9,10},{10,11},{12,13},{... | collective-permute-start | bytes 221192 | tf_op jit(solution)/shard_map/ppermute | solution.py:18
  7.0 6.6 %collective-permute-start.1 = (bf16[1,2,288,128]{2,3,1,0:T(8,128)(2,1)S(1)}, bf16[1,2,288,128]{2,3,1,0:T(8,128)(2,1)S(1)}, u32[]{:S(2)}, u32[]{:S(2)}) collective-permute-start(bf16[1,2,288,128]{2,3,1,0:T(8,128)(2,1)S(1)} %get-tuple-element.38), channel_id=1, source_target_pairs={{0,4},{4,8},{8,12},{12,16},{16,20},{20,24},{24,28},{1,5},{5,9},{9,... | collective-permute-start | bytes 442376 | tf_op jit(solution)/shard_map/ppermute | solution.py:18
  14.2 4.4 %copy-start.1 = (bf16[1,2,1152,1152]{3,2,1,0:T(8,128)(2,1)S(1)}, bf16[1,2,1152,1152]{3,2,1,0:T(8,128)(2,1)}, u32[]{:S(2)}) copy-start(bf16[1,2,1152,1152]{3,2,1,0:T(8,128)(2,1)} %param.13) | copy-start | bytes 15925252
  20.5 6.4 %collective-permute-start.2 = (f32[1,1,288,128]{2,3,1,0:T(8,128)S(1)}, f32[1,1,288,128]{2,3,1,0:T(8,128)S(1)}, u32[]{:S(2)}, u32[]{:S(2)}) collective-permute-start(f32[1,1,288,128]{2,3,1,0:T(8,128)S(1)} %get-tuple-element.29), channel_id=1, source_target_pairs={{1,0},{2,1},{3,2},{5,4},{6,5},{7,6},{9,8},{10,9},{11,10},{13,12},{... | collective-permute-start | bytes 442376 | tf_op jit(solution)/shard_map/ppermute | solution.py:18
  27.1 11.3 %collective-permute-start.3 = (f32[1,2,288,128]{2,3,1,0:T(8,128)S(1)}, f32[1,2,288,128]{2,3,1,0:T(8,128)S(1)}, u32[]{:S(2)}, u32[]{:S(2)}) collective-permute-start(f32[1,2,288,128]{2,3,1,0:T(8,128)S(1)} %get-tuple-element.27), channel_id=1, source_target_pairs={{4,0},{8,4},{12,8},{16,12},{20,16},{24,20},{28,24},{5,1},{9,5},{13... | collective-permute-start | bytes 884744 | tf_op jit(solution)/shard_map/ppermute | solution.py:18
  38.5 86.8 %slice-start = ((s8[5308416]{0:T(1024)(128)(4,1)}), s8[1114112]{0:T(1024)(128)(4,1)S(1)}, s32[]{:S(2)}) async-start(s8[5308416]{0:T(1024)(128)(4,1)} %bitcast.171), calls=%async_computation | async-start | bytes 2228224
  38.6 8.5 %copy-start.3 = (bf16[1,2,288,128]{2,3,1,0:T(8,128)(2,1)}, bf16[1,2,288,128]{2,3,1,0:T(8,128)(2,1)S(1)}, u32[]{:S(2)}) copy-start(bf16[1,2,288,128]{2,3,1,0:T(8,128)(2,1)S(1)} %get-tuple-element.36) | copy-start | bytes 442372
  39.3 6.0 %collective-permute-start.4 = (bf16[1,1,288,128]{2,3,1,0:T(8,128)(2,1)}, bf16[1,1,288,128]{2,3,1,0:T(8,128)(2,1)S(1)}, u32[]{:S(2)}, u32[]{:S(2)}) collective-permute-start(bf16[1,1,288,128]{2,3,1,0:T(8,128)(2,1)} %get-tuple-element.46), channel_id=1, source_target_pairs={{0,1},{1,2},{2,3},{4,5},{5,6},{6,7},{8,9},{9,10},{10,11},{12,13},{... | collective-permute-start | bytes 221192 | tf_op jit(solution)/shard_map/ppermute | solution.py:18
  42.5 4.6 %collective-permute-start.5 = (bf16[1,2,288,128]{2,3,1,0:T(8,128)(2,1)S(1)}, bf16[1,2,288,128]{2,3,1,0:T(8,128)(2,1)S(1)}, u32[]{:S(2)}, u32[]{:S(2)}) collective-permute-start(bf16[1,2,288,128]{2,3,1,0:T(8,128)(2,1)S(1)} %get-tuple-element.36), channel_id=1, source_target_pairs={{0,4},{4,8},{8,12},{12,16},{16,20},{20,24},{24,28},{1,5},{5,9},{9,... | collective-permute-start | bytes 442376 | tf_op jit(solution)/shard_map/ppermute | solution.py:18
  120.5 4.8 %slice-start.1 = ((s8[5308416]{0:T(1024)(128)(4,1)}), s8[4194304]{0:T(1024)(128)(4,1)S(1)}, s32[]{:S(2)}) async-start(s8[5308416]{0:T(1024)(128)(4,1)} %bitcast.171), calls=%async_computation.1 | async-start | bytes 8388608
  127.2 8.2 %collective-permute-start.6 = (f32[1,1,288,128]{2,3,1,0:T(8,128)S(1)}, f32[1,1,288,128]{2,3,1,0:T(8,128)S(1)}, u32[]{:S(2)}, u32[]{:S(2)}) collective-permute-start(f32[1,1,288,128]{2,3,1,0:T(8,128)S(1)} %get-tuple-element.25), channel_id=1, source_target_pairs={{1,0},{2,1},{3,2},{5,4},{6,5},{7,6},{9,8},{10,9},{11,10},{13,12},{... | collective-permute-start | bytes 442376 | tf_op jit(solution)/shard_map/ppermute | solution.py:18
  135.6 9.9 %collective-permute-start.7 = (f32[1,2,288,128]{2,3,1,0:T(8,128)S(1)}, f32[1,2,288,128]{2,3,1,0:T(8,128)S(1)}, u32[]{:S(2)}, u32[]{:S(2)}) collective-permute-start(f32[1,2,288,128]{2,3,1,0:T(8,128)S(1)} %get-tuple-element.23), channel_id=1, source_target_pairs={{4,0},{8,4},{12,8},{16,12},{20,16},{24,20},{28,24},{5,1},{9,5},{13... | collective-permute-start | bytes 884744 | tf_op jit(solution)/shard_map/ppermute | solution.py:18
  145.9 3.4 %collective-permute-start.8 = (bf16[1,1,288,128]{2,3,1,0:T(8,128)(2,1)S(1)}, bf16[1,1,288,128]{2,3,1,0:T(8,128)(2,1)S(1)}, u32[]{:S(2)}, u32[]{:S(2)}) collective-permute-start(bf16[1,1,288,128]{2,3,1,0:T(8,128)(2,1)S(1)} %get-tuple-element.44), channel_id=1, source_target_pairs={{0,1},{1,2},{2,3},{4,5},{5,6},{6,7},{8,9},{9,10},{10,11},{12,13},{... | collective-permute-start | bytes 221192 | tf_op jit(solution)/shard_map/ppermute | solution.py:18
  147.4 4.5 %collective-permute-start.9 = (bf16[1,2,288,128]{2,3,1,0:T(8,128)(2,1)S(1)}, bf16[1,2,288,128]{2,3,1,0:T(8,128)(2,1)S(1)}, u32[]{:S(2)}, u32[]{:S(2)}) collective-permute-start(bf16[1,2,288,128]{2,3,1,0:T(8,128)(2,1)S(1)} %get-tuple-element.34), channel_id=1, source_target_pairs={{0,4},{4,8},{8,12},{12,16},{16,20},{20,24},{24,28},{1,5},{5,9},{9,... | collective-permute-start | bytes 442376 | tf_op jit(solution)/shard_map/ppermute | solution.py:18
  161.1 7.9 %collective-permute-start.10 = (f32[1,1,288,128]{2,3,1,0:T(8,128)S(1)}, f32[1,1,288,128]{2,3,1,0:T(8,128)S(1)}, u32[]{:S(2)}, u32[]{:S(2)}) collective-permute-start(f32[1,1,288,128]{2,3,1,0:T(8,128)S(1)} %get-tuple-element.21), channel_id=1, source_target_pairs={{1,0},{2,1},{3,2},{5,4},{6,5},{7,6},{9,8},{10,9},{11,10},{13,12},{... | collective-permute-start | bytes 442376 | tf_op jit(solution)/shard_map/ppermute | solution.py:18
  169.2 10.3 %collective-permute-start.11 = (f32[1,2,288,128]{2,3,1,0:T(8,128)S(1)}, f32[1,2,288,128]{2,3,1,0:T(8,128)S(1)}, u32[]{:S(2)}, u32[]{:S(2)}) collective-permute-start(f32[1,2,288,128]{2,3,1,0:T(8,128)S(1)} %get-tuple-element.19), channel_id=1, source_target_pairs={{4,0},{8,4},{12,8},{16,12},{20,16},{24,20},{28,24},{5,1},{9,5},{13... | collective-permute-start | bytes 884744 | tf_op jit(solution)/shard_map/ppermute | solution.py:18
  180.8 4.5 %collective-permute-start.12 = (bf16[1,1,288,128]{2,3,1,0:T(8,128)(2,1)S(1)}, bf16[1,1,288,128]{2,3,1,0:T(8,128)(2,1)S(1)}, u32[]{:S(2)}, u32[]{:S(2)}) collective-permute-start(bf16[1,1,288,128]{2,3,1,0:T(8,128)(2,1)S(1)} %get-tuple-element.42), channel_id=1, source_target_pairs={{0,1},{1,2},{2,3},{4,5},{5,6},{6,7},{8,9},{9,10},{10,11},{12,13},{... | collective-permute-start | bytes 221192 | tf_op jit(solution)/shard_map/ppermute | solution.py:18
  183.4 4.5 %collective-permute-start.13 = (bf16[1,2,288,128]{2,3,1,0:T(8,128)(2,1)S(1)}, bf16[1,2,288,128]{2,3,1,0:T(8,128)(2,1)S(1)}, u32[]{:S(2)}, u32[]{:S(2)}) collective-permute-start(bf16[1,2,288,128]{2,3,1,0:T(8,128)(2,1)S(1)} %get-tuple-element.32), channel_id=1, source_target_pairs={{0,4},{4,8},{8,12},{12,16},{16,20},{20,24},{24,28},{1,5},{5,9},{9,... | collective-permute-start | bytes 442376 | tf_op jit(solution)/shard_map/ppermute | solution.py:18
  188.8 44.3 %copy-start.4 = (bf16[32,64]{1,0:T(8,128)(2,1)S(1)}, bf16[32,64]{1,0:T(8,128)(2,1)}, u32[]{:S(2)}) copy-start(bf16[32,64]{1,0:T(8,128)(2,1)} %param.16) | copy-start | bytes 12292
  266.7 8.2 %collective-permute-start.14 = (f32[1,1,288,128]{2,3,1,0:T(8,128)S(1)}, f32[1,1,288,128]{2,3,1,0:T(8,128)S(1)}, u32[]{:S(2)}, u32[]{:S(2)}) collective-permute-start(f32[1,1,288,128]{2,3,1,0:T(8,128)S(1)} %get-tuple-element.17), channel_id=1, source_target_pairs={{1,0},{2,1},{3,2},{5,4},{6,5},{7,6},{9,8},{10,9},{11,10},{13,12},{... | collective-permute-start | bytes 442376 | tf_op jit(solution)/shard_map/ppermute | solution.py:18
  275.0 9.9 %collective-permute-start.15 = (f32[1,2,288,128]{2,3,1,0:T(8,128)S(1)}, f32[1,2,288,128]{2,3,1,0:T(8,128)S(1)}, u32[]{:S(2)}, u32[]{:S(2)}) collective-permute-start(f32[1,2,288,128]{2,3,1,0:T(8,128)S(1)} %get-tuple-element.15), channel_id=1, source_target_pairs={{4,0},{8,4},{12,8},{16,12},{20,16},{24,20},{28,24},{5,1},{9,5},{13... | collective-permute-start | bytes 884744 | tf_op jit(solution)/shard_map/ppermute | solution.py:18
  285.4 3.4 %collective-permute-start.16 = (bf16[1,1,288,128]{2,3,1,0:T(8,128)(2,1)S(1)}, bf16[1,1,288,128]{2,3,1,0:T(8,128)(2,1)S(1)}, u32[]{:S(2)}, u32[]{:S(2)}) collective-permute-start(bf16[1,1,288,128]{2,3,1,0:T(8,128)(2,1)S(1)} %get-tuple-element.40), channel_id=1, source_target_pairs={{0,1},{1,2},{2,3},{4,5},{5,6},{6,7},{8,9},{9,10},{10,11},{12,13},{... | collective-permute-start | bytes 221192 | tf_op jit(solution)/shard_map/ppermute | solution.py:18
  286.9 4.5 %collective-permute-start.17 = (bf16[1,2,288,128]{2,3,1,0:T(8,128)(2,1)S(1)}, bf16[1,2,288,128]{2,3,1,0:T(8,128)(2,1)S(1)}, u32[]{:S(2)}, u32[]{:S(2)}) collective-permute-start(bf16[1,2,288,128]{2,3,1,0:T(8,128)(2,1)S(1)} %get-tuple-element.30), channel_id=1, source_target_pairs={{0,4},{4,8},{8,12},{12,16},{16,20},{20,24},{24,28},{1,5},{5,9},{9,... | collective-permute-start | bytes 442376 | tf_op jit(solution)/shard_map/ppermute | solution.py:18
  300.6 10.2 %copy-start.2 = (f32[1,2,2,288,128]{3,4,1,2,0:T(8,128)S(1)}, f32[1,2,2,288,128]{3,4,1,2,0:T(8,128)}, u32[]{:S(2)}) copy-start(f32[1,2,2,288,128]{3,4,1,2,0:T(8,128)} %get-tuple-element.9) | copy-start | bytes 1769476
  300.6 8.1 %collective-permute-start.18 = (f32[1,1,288,128]{2,3,1,0:T(8,128)S(1)}, f32[1,1,288,128]{2,3,1,0:T(8,128)S(1)}, u32[]{:S(2)}, u32[]{:S(2)}) collective-permute-start(f32[1,1,288,128]{2,3,1,0:T(8,128)S(1)} %get-tuple-element.13), channel_id=1, source_target_pairs={{1,0},{2,1},{3,2},{5,4},{6,5},{7,6},{9,8},{10,9},{11,10},{13,12},{... | collective-permute-start | bytes 442376 | tf_op jit(solution)/shard_map/ppermute | solution.py:18
  308.8 10.1 %collective-permute-start.19 = (f32[1,2,288,128]{2,3,1,0:T(8,128)S(1)}, f32[1,2,288,128]{2,3,1,0:T(8,128)S(1)}, u32[]{:S(2)}, u32[]{:S(2)}) collective-permute-start(f32[1,2,288,128]{2,3,1,0:T(8,128)S(1)} %get-tuple-element.11), channel_id=1, source_target_pairs={{4,0},{8,4},{12,8},{16,12},{20,16},{24,20},{28,24},{5,1},{9,5},{13... | collective-permute-start | bytes 884744 | tf_op jit(solution)/shard_map/ppermute | solution.py:18
where the time goes:
time: 321 us; the launch traced here: 320 us
  blocking collectives  138 us (43%)
  waiting for transfers between devices  81.7 us (25%)
  starting transfers between devices  42.9 us (13%)
  matrix products  40.8 us (13%)
  local copies, waits for them, and re-layouts  10.5 us (3%)
  other arithmetic  5.31 us (2%)
    ppermute x20, waiting for transfers between devices, from_behind(): return lax.ppermute(shard, axis, pairs)  81.7 us
    psum x2, blocking collectives, coarse_term(): totals = lax.psum(placed, ('sx', 'sy'))  80.9 us
    ppermute x20, starting transfers between devices, from_behind(): return lax.ppermute(shard, axis, pairs)  42.9 us
    all_gather x2, blocking collectives, coarse_term(): lax.all_gather(solved, 'sx', axis=0, tiled=True)  30.1 us
    psum x2, blocking collectives, coarse_term(): solved = lax.psum(row_part, 'sy').astype(jnp.bfloat16)  26.7 us
    dot_general x5, matrix products, paired(): jnp.einsum('rsij,rsjl->rsil', wrinkle, vectors, preferred_element_type=jn...  21.4 us
    dot_general x5, matrix products, paired(): jnp.einsum('rsij,rsjl->rsil', taut, vectors, preferred_element_type=jnp.f...  16.1 us
  transfers between devices with their start and end apart: 20, of which 15 were waited for; matrix products, arithmetic and copies ran while one was open for 1% of the time, Pallas kernels for 0%

commit v1 on v0

v1 whole, which is shorter than its diff:
```python
import functools

import jax
import jax.numpy as jnp
from jax import lax
from jax.experimental import pallas as pl
from jax.experimental.pallas import tpu as pltpu
from jax.sharding import PartitionSpec as P

ITERS = 2
step_sizes = (0.55, 0.75)
momenta = (0.0, 0.15)

MESH = pl.DeviceIdType.MESH
SLOT = 16
F32 = jnp.float32
BF16 = jnp.bfloat16


def kernel(
    nr, ns,
    loads_ref, dual_t, dual_w, diri_t, diri_w, coup_ref, cinv_ref, wr_ref, len_ref, cm_ref,
    mult_out, prec_out,
    am, aw, bm, bw, vec, loc, snd, rcv, ld, mu, di, cpad, meta, mz, mx, cf, kmat, ts, tp, ys, yr,
    mat_sem, h_send, h_recv, mz_send, mz_recv, mx_send, mx_recv, cz_send, cz_recv, cx_send, cx_recv,
    t_send, t_recv, y_send, y_recv,
):
    r, s = lax.axis_index("sx"), lax.axis_index("sy")
    per = loads_ref.shape[1]
    edge, width = loads_ref.shape[3], loads_ref.shape[4]
    corners = coup_ref.shape[2]
    tr, tc = cinv_ref.shape
    order = nr * tr
    rows = per * SLOT
    has_left, has_right = s > 0, s < ns - 1
    has_up, has_down = r > 0, r < nr - 1
    FROM_LEFT, FROM_RIGHT, FROM_UP, FROM_DOWN = 0, 1, 2, 2 + per

    loads_in = []
    for i, (src, dst) in enumerate(((diri_t, am), (diri_w, aw), (dual_t, bm), (dual_w, bw))):
        for c in range(per):
            loads_in.append(pltpu.make_async_copy(src.at[0, c], dst.at[c], mat_sem.at[i * per + c]))
    for c in range(per):
        for i in (0, 1):
            loads_in[i * per + c].start()
    for c in range(per):
        for i in (2, 3):
            loads_in[i * per + c].start()

    barrier = pltpu.get_barrier_semaphore()
    for k in range(1, nr):
        pl.semaphore_signal(barrier, inc=1, device_id={"sx": lax.rem(r + k, nr)}, device_id_type=MESH)
    for k in range(1, ns):
        pl.semaphore_signal(barrier, inc=1, device_id={"sy": lax.rem(s + k, ns)}, device_id_type=MESH)

    meta[...] = jnp.full(meta.shape, -1, jnp.int32)
    for c in range(per):
        for m in range(corners):
            meta[c * SLOT + m : c * SLOT + m + 1, :] = jnp.full((1, 128), cm_ref[0, c, m], jnp.int32)
        east = len_ref[0, c, 0]
        if c == per - 1:
            east = jnp.where(has_right, east, 0)
        south = jnp.where(has_down, len_ref[0, c, 1], 0)
        meta[rows + c : rows + c + 1, :] = jnp.full((1, 128), east, jnp.int32)
        meta[rows + per + c : rows + per + c + 1, :] = jnp.full((1, 128), south, jnp.int32)
    mz[pl.ds(s, 1)] = meta[...][None]
    mx[pl.ds(r, 1)] = meta[...][None]
    cf[pl.ds(s, 1), pl.ds(pl.multiple_of(r * tr, 8), tr), :] = cinv_ref[...].astype(F32)[None]

    positions = lax.broadcasted_iota(jnp.int32, (edge, width), 0)

    def live(length_row):
        return positions < jnp.broadcast_to(length_row, (edge, width))

    own_mask = {}
    for c in range(per):
        own_mask[c] = meta[rows + c : rows + c + 1, :]
        own_mask[per + c] = meta[rows + per + c : rows + per + c + 1, :]

    EAST, SOUTH, NORTH, WEST = 0, per, 2 * per, 3 * per

    def halo(k, slot, where_to):
        axis, shift = where_to
        index = (r if axis == "sx" else s) + shift
        return pltpu.make_async_remote_copy(
            src_ref=snd.at[k, slot], dst_ref=rcv.at[k, slot],
            send_sem=h_send.at[k, slot], recv_sem=h_recv.at[k, slot],
            device_id={axis: index}, device_id_type=MESH,
        )

    def route(slot):
        if slot == FROM_LEFT:
            return ("sy", 1), has_right, has_left
        if slot == FROM_RIGHT:
            return ("sy", -1), has_left, has_right
        if slot < FROM_DOWN:
            return ("sx", 1), has_down, has_up
        return ("sx", -1), has_up, has_down

    def send(k, slot, value):
        snd[k, slot] = value.astype(BF16)
        to, can, _ = route(slot)

        @pl.when(can)
        def _():
            halo(k, slot, to).start()

    def arrive(k, slot):
        to, _, gets = route(slot)

        @pl.when(gets)
        def _():
            halo(k, slot, to).wait_recv()

    def left_behind(k, slot):
        to, can, _ = route(slot)

        @pl.when(can)
        def _():
            halo(k, slot, to).wait_send()

    def put(kind, c, value):
        value = value.astype(BF16)
        if kind == EAST:
            vec[c, 0:edge] = value
            if c + 1 < per:
                vec[c + 1, 2 * edge : 3 * edge] = -value
        elif kind == SOUTH:
            vec[c, edge : 2 * edge] = value
        elif kind == NORTH:
            vec[c, 3 * edge :] = -value
        else:
            vec[0, 2 * edge : 3 * edge] = -value

    for c in range(per):
        for kind in (0, 1):
            e = kind * per + c
            value = jnp.where(live(own_mask[e]), loads_ref[0, c, kind], 0.0)
            ld[e] = value
            put(EAST if kind == 0 else SOUTH, c, 0.5 * value)
            if kind == 1:
                snd[0, FROM_UP + c] = value.astype(BF16)
            elif c == per - 1:
                snd[0, FROM_LEFT] = value.astype(BF16)
    pl.semaphore_wait(barrier, nr - 1 + ns - 1)
    for slot in [FROM_LEFT] + [FROM_UP + c for c in range(per)]:
        to, can, _ = route(slot)

        @pl.when(can)
        def _(to=to, slot=slot):
            halo(0, slot, to).start()

    def peer_copy(axis, k, src, dst, ssem, rsem):
        n, me = (nr, r) if axis == "sx" else (ns, s)
        return pltpu.make_async_remote_copy(
            src_ref=src, dst_ref=dst, send_sem=ssem.at[k], recv_sem=rsem.at[k],
            device_id={axis: lax.rem(me + k, n)}, device_id_type=MESH,
        )

    my_rows = pl.ds(pl.multiple_of(r * tr, 8), tr)
    cz = [peer_copy("sy", k, cf.at[s, my_rows], cf.at[s, my_rows], cz_send, cz_recv) for k in range(1, ns)]
    mzc = [peer_copy("sy", k, meta, mz.at[s], mz_send, mz_recv) for k in range(1, ns)]
    mxc = [peer_copy("sx", k, meta, mx.at[r], mx_send, mx_recv) for k in range(1, nr)]
    cx = [peer_copy("sx", k, cf.at[:, my_rows], cf.at[:, my_rows], cx_send, cx_recv) for k in range(1, nr)]
    for copy in cz + mzc + mxc:
        copy.start()

    cpad[...] = jnp.zeros(cpad.shape, BF16)
    for c in range(per):
        cpad[c, 0:corners] = coup_ref[0, c]

    def combine(c, main, extra):
        flag = jnp.full((1, 1), wr_ref[0, c], jnp.int32).astype(F32).astype(BF16)
        size = main.shape[1]
        step = 128

        def body(i, _):
            part = pl.ds(pl.multiple_of(i * step, step), step)
            main[c, part] = main[c, part] + flag * extra[c, part]
            return 0

        lax.fori_loop(0, size // step, body, 0)

    def product(mat, c, e):
        return jnp.dot(mat[c, e * edge : (e + 1) * edge, :], vec[c], preferred_element_type=F32)

    blocks = [(c, 3) for c in range(per)] + [(c, 1) for c in range(per)]
    blocks += [(per - 1, 0), (0, 2)]
    blocks += [(c, 0) for c in range(per - 1)] + [(c, 2) for c in range(1, per)]

    def slot_of(c, e):
        if e == 3:
            return FROM_DOWN + c
        if e == 1:
            return FROM_UP + c
        if e == 0 and c == per - 1:
            return FROM_LEFT
        if e == 2 and c == 0:
            return FROM_RIGHT
        return None

    def deliver(k, c, e, value, last):
        loc[c, e * edge : (e + 1) * edge] = value
        slot = slot_of(c, e)
        if slot is not None and not (last and e in (0, 1)):
            send(k, slot, value)

    def local_rows(c, e):
        return loc[c, e * edge : (e + 1) * edge]

    def mask_of(kind, c):
        if kind == EAST:
            return live(own_mask[c])
        if kind == SOUTH:
            return live(own_mask[per + c])
        if kind == NORTH:
            row = mx[jnp.maximum(r - 1, 0), rows + per + c : rows + per + c + 1, :]
            return live(jnp.where(has_up, row, 0))
        row = mz[jnp.maximum(s - 1, 0), rows + per - 1 : rows + per, :]
        return live(jnp.where(has_left, row, 0))

    def gathered(k, kind, c):
        if kind == EAST:
            if c + 1 < per:
                return local_rows(c, 0) - local_rows(c + 1, 2)
            arrive(k, FROM_RIGHT)
            return local_rows(c, 0) - rcv[k, FROM_RIGHT].astype(F32)
        if kind == SOUTH:
            arrive(k, FROM_DOWN + c)
            return local_rows(c, 1) - rcv[k, FROM_DOWN + c].astype(F32)
        if kind == NORTH:
            arrive(k, FROM_UP + c)
            return rcv[k, FROM_UP + c].astype(F32) - local_rows(c, 3)
        arrive(k, FROM_LEFT)
        return rcv[k, FROM_LEFT].astype(F32) - local_rows(0, 2)

    inner = [(EAST, c) for c in range(per)]
    everything = inner + [(WEST, 0)] + [(SOUTH, c) for c in range(per)] + [(NORTH, c) for c in range(per)]

    for c in range(per):
        loads_in[c].wait()
        loads_in[per + c].wait()
        combine(c, am, aw)
    for slot, kind, c, there in [(FROM_LEFT, WEST, 0, has_left)] + [(FROM_UP + c, NORTH, c, has_up) for c in range(per)]:
        arrive(0, slot)
        value = jnp.where(jnp.broadcast_to(there, (edge, width)), rcv[0, slot].astype(F32), 0.0)
        ld[kind + c] = value
        put(kind, c, 0.5 * value)

    def setup_middle():
        for k in range(ns - 1):
            cz[k].wait_recv()
            mzc[k].wait_recv()
        for copy in cx:
            copy.start()
        for k in range(nr - 1):
            mxc[k].wait_recv()

    def setup_end():
        for k in range(nr - 1):
            cx[k].wait_recv()
        row_index = mz[:, 0:rows, :].reshape(ns * rows, 128)[:, 0:1]
        plane_index = mx[:, 0:rows, :].reshape(nr * rows, 128)[:, 0:1]
        row_pick = (
            jnp.broadcast_to(row_index, (ns * rows, order))
            == lax.broadcasted_iota(jnp.int32, (ns * rows, order), 1)
        ).astype(F32).astype(BF16)
        total = jnp.zeros((ns * rows, nr * rows), F32)
        for q in range(ns):
            picked = jnp.dot(row_pick, cf[q].astype(BF16), preferred_element_type=F32).astype(BF16)
            plane_pick = (
                jnp.broadcast_to(plane_index, (nr * rows, tc))
                == lax.broadcasted_iota(jnp.int32, (nr * rows, tc), 1) + q * tc
            ).astype(F32).astype(BF16)
            total = total + lax.dot_general(
                picked, plane_pick, (((1,), (1,)), ((), ())), preferred_element_type=F32
            )
        kmat[...] = total.astype(BF16)

    halo_round = 1
    for number in range(ITERS):
        for c, e in blocks:
            deliver(halo_round, c, e, product(am, c, e), False)
        if number == 0:
            setup_middle()
            for c in range(per):
                loads_in[2 * per + c].wait()
                loads_in[3 * per + c].wait()
                combine(c, bm, bw)
            setup_end()
        for kind, c in everything:
            value = jnp.where(mask_of(kind, c), 0.5 * gathered(halo_round, kind, c), 0.0)
            if number == 0:
                iterate = step_sizes[0] * value
            else:
                value = value + momenta[number] * di[kind + c]
                iterate = mu[kind + c] + step_sizes[number] * value
            if number < ITERS - 1:
                di[kind + c] = value
                mu[kind + c] = iterate
            elif kind in (EAST, SOUTH):
                mult_out[0, c, 0 if kind == EAST else 1] = iterate
            put(kind, c, iterate)
        halo_round += 1

        for c in range(per):
            terms = jnp.dot(cpad[c], vec[c], preferred_element_type=F32).astype(BF16)
            ts[number, c * SLOT : (c + 1) * SLOT] = terms
            tp[number, pl.ds(r, 1), c * SLOT : (c + 1) * SLOT] = terms[None]
        tcopies = [
            peer_copy("sx", k, ts.at[number], tp.at[number, r], t_send.at[number], t_recv.at[number])
            for k in range(1, nr)
        ]
        for copy in tcopies:
            copy.start()
        half = len(blocks) // 2
        for c, e in blocks[:half]:
            loc[c, e * edge : (e + 1) * edge] = product(bm, c, e)
        for copy in tcopies:
            copy.wait_recv()
        partial = jnp.dot(kmat[...], tp[number].reshape(nr * rows, 128), preferred_element_type=F32)
        ys[number] = partial.astype(BF16).reshape(ns, rows, 128)
        yr[number, pl.ds(s, 1)] = ys[number, pl.ds(s, 1)]
        ycopies = [
            peer_copy(
                "sy", k, ys.at[number, lax.rem(s + k, ns)], yr.at[number, s],
                y_send.at[number], y_recv.at[number],
            )
            for k in range(1, ns)
        ]
        for copy in ycopies:
            copy.start()
        for c, e in blocks[half:]:
            loc[c, e * edge : (e + 1) * edge] = product(bm, c, e)
        for copy in ycopies:
            copy.wait_recv()
        solved = yr[number, 0].astype(F32)
        for q in range(1, ns):
            solved = solved + yr[number, q].astype(F32)
        solved = solved.astype(BF16)
        for c, e in blocks:
            coarse = lax.dot_general(
                cpad[c, :, e * edge : (e + 1) * edge] if (e * edge) % 128 == 0 and edge % 128 == 0 else cpad[c][:, e * edge : (e + 1) * edge],
                solved[c * SLOT : (c + 1) * SLOT], (((0,), (0,)), ((), ())), preferred_element_type=F32,
            )
            deliver(halo_round, c, e, local_rows(c, e) + coarse, False)
        for kind, c in everything:
            value = jnp.where(mask_of(kind, c), gathered(halo_round, kind, c), 0.0)
            put(kind, c, 0.5 * (ld[kind + c] - value))
        halo_round += 1
        for copy in tcopies + ycopies:
            copy.wait_send()

    for c, e in blocks:
        deliver(halo_round, c, e, product(am, c, e), True)
    for c in range(per):
        for kind in (EAST, SOUTH):
            value = jnp.where(mask_of(kind, c), 0.5 * gathered(halo_round, kind, c), 0.0)
            prec_out[0, c, 0 if kind == EAST else 1] = value

    for copy in cz + mzc + mxc + cx:
        copy.wait_send()
    down_right = [FROM_LEFT] + [FROM_UP + c for c in range(per)]
    up_left = [FROM_RIGHT] + [FROM_DOWN + c for c in range(per)]
    for k in range(halo_round + 1):
        slots = down_right if k == 0 else up_left if k == halo_round else down_right + up_left
        for slot in slots:
            left_behind(k, slot)


def local(nr, ns, *args):
    adjoint_loads, dual_taut, coupling, coarse_inverse = args[0], args[1], args[5], args[6]
    per, edge, width = adjoint_loads.shape[1], adjoint_loads.shape[3], adjoint_loads.shape[4]
    size = dual_taut.shape[-1]
    tr, tc = coarse_inverse.shape
    rows = per * SLOT
    rounds = 2 * ITERS + 2
    slots = 2 + 2 * per
    meta_rows = rows + -(-2 * per // 8) * 8
    dma = pltpu.SemaphoreType.DMA
    vmem = pl.BlockSpec(memory_space=pltpu.VMEM)
    smem = pl.BlockSpec(memory_space=pltpu.SMEM)
    hbm = pl.BlockSpec(memory_space=pl.ANY)
    mats = [pltpu.VMEM((per, size, size), BF16)] * 4
    scratch = mats + [
        pltpu.VMEM((per, size, width), BF16),
        pltpu.VMEM((per, size, width), F32),
        pltpu.VMEM((rounds, slots, edge, width), BF16),
        pltpu.VMEM((rounds, slots, edge, width), BF16),
        pltpu.VMEM((3 * per + 1, edge, width), F32),
        pltpu.VMEM((3 * per + 1, edge, width), F32),
        pltpu.VMEM((3 * per + 1, edge, width), F32),
        pltpu.VMEM((per, SLOT, size), BF16),
        pltpu.VMEM((meta_rows, 128), jnp.int32),
        pltpu.VMEM((ns, meta_rows, 128), jnp.int32),
        pltpu.VMEM((nr, meta_rows, 128), jnp.int32),
        pltpu.VMEM((ns, nr * tr, tc), F32),
        pltpu.VMEM((ns * rows, nr * rows), BF16),
        pltpu.VMEM((ITERS, rows, width), BF16),
        pltpu.VMEM((ITERS, nr, rows, width), BF16),
        pltpu.VMEM((ITERS, ns, rows, width), BF16),
        pltpu.VMEM((ITERS, ns, rows, width), BF16),
        dma((4 * per,)),
        dma((rounds, slots)), dma((rounds, slots)),
        dma((ns,)), dma((ns,)),
        dma((nr,)), dma((nr,)),
        dma((ns,)), dma((ns,)),
        dma((nr,)), dma((nr,)),
        dma((ITERS, nr)), dma((ITERS, nr)),
        dma((ITERS, ns)), dma((ITERS, ns)),
    ]
    out = jax.ShapeDtypeStruct(adjoint_loads.shape, F32)
    return pl.pallas_call(
        functools.partial(kernel, nr, ns),
        out_shape=(out, out),
        in_specs=[vmem, hbm, hbm, hbm, hbm, vmem, vmem, smem, smem, smem],
        out_specs=(vmem, vmem),
        scratch_shapes=scratch,
        compiler_params=pltpu.CompilerParams(
            collective_id=0, has_side_effects=True, vmem_limit_bytes=60 * 1024 * 1024
        ),
    )(*args)


def solution(mesh):
    placed = (
        P("sx", "sy", None, None, None),
        P("sx", "sy", None, None),
        P("sx", "sy", None, None),
        P("sx", "sy", None, None),
        P("sx", "sy", None, None),
        P("sx", "sy", None, None),
        P("sx", "sy"),
        P("sx", "sy"),
        P("sx", "sy", None),
        P("sx", "sy", None),
    )
    return jax.shard_map(
        functools.partial(local, mesh.shape["sx"], mesh.shape["sy"]),
        mesh=mesh,
        in_specs=placed,
        out_specs=(P("sx", "sy", None, None, None), P("sx", "sy", None, None, None)),
        check_vma=False,
    )
```

time: 321 us -> 66.5 us (0.21)
  the two profiles are of different devices: /device:TPU:1 before, /device:TPU:0 now
where the time goes in v1:
time: 66.5 us; the launch traced here: 66.2 us
  Pallas kernels  60.3 us (91%)
  local copies, waits for them, and re-layouts  5.29 us (8%)
    pallas_call x1, Pallas kernels, local(): pl.pallas_call(functools.partial(kernel, nr, ns), out_shape=(out, out), i...  60.3 us
    unnamed x3, local copies, waits for them, and re-layouts  5.29 us

profile of v1, /device:TPU:0, one launch (start us, length us, event | category | flops | bytes accessed | tf_op | source)
XLA Modules:
  0.0 66.2 jit_solution(10801115576165596066)
XLA Ops:
  0.6 1.5 %copy.12.coup_ref = bf16[1,2,12,1152]{3,2,1,0:T(8,128)(2,1)} copy(bf16[1,2,12,1152]{3,1,2,0:T(2,128)(2,1)} %param.15) | data formatting | bytes 110592 | tf_op args[5]
  2.1 60.3 %shard_map.113 = (f32[1,2,2,288,128]{4,3,2,1,0:T(8,128)}, f32[1,2,2,288,128]{4,3,2,1,0:T(8,128)}) custom-call(f32[1,2,2,288,128]{4,3,2,1,0:T(8,128)} %loads_ref.1, bf16[1,2,1152,1152]{3,2,1,0:T(8,128)(2,1)} %dual_t.1, bf16[1,2,1152,1152]{3,2,1,0:T(8,128)(2,1)} %dual_w.1, bf16[1,2,1152,1152]{3,2,1,0:T(8,128)(2,1)} %diri_t.1, ...), custom_call_target="tpu_custom_call" | custom-call | tf_op jit(solution)/shard_map/pallas_call | solution.py:413
  62.4 1.9 %copy.15 = f32[1,2,2,288,128]{4,3,2,1,0:T(8,128)} copy(f32[1,2,2,288,128]{4,3,2,1,0:T(8,128)} %get-tuple-element.4) | data formatting | bytes 1179648
  64.3 1.9 %copy.16 = f32[1,2,2,288,128]{4,3,2,1,0:T(8,128)} copy(f32[1,2,2,288,128]{4,3,2,1,0:T(8,128)} %get-tuple-element.5) | data formatting | bytes 1179648

commit v2 on v1

--- a/solution.py
+++ b/solution.py
@@ -21,14 +21,14 @@
     nr, ns,
     loads_ref, dual_t, dual_w, diri_t, diri_w, coup_ref, cinv_ref, wr_ref, len_ref, cm_ref,
     mult_out, prec_out,
-    am, aw, bm, bw, vec, loc, snd, rcv, ld, mu, di, cpad, meta, mz, mx, cf, kmat, ts, tp, ys, yr,
+    am, aw, bm, bw, vec, loc, snd, rcv, ld, mu, di, cpad, ncp, ct, nct, meta, mz, mx, cf, kmat, ts, tp, ys, yr, yo, yn,
     mat_sem, h_send, h_recv, mz_send, mz_recv, mx_send, mx_recv, cz_send, cz_recv, cx_send, cx_recv,
-    t_send, t_recv, y_send, y_recv,
+    t_send, t_recv, y_send, y_recv, c_send, c_recv, n_send, n_recv,
 ):
     r, s = lax.axis_index("sx"), lax.axis_index("sy")
     per = loads_ref.shape[1]
     edge, width = loads_ref.shape[3], loads_ref.shape[4]
-    corners = coup_ref.shape[2]
+    corners = coup_ref.shape[1]
     tr, tc = cinv_ref.shape
     order = nr * tr
     rows = per * SLOT
@@ -43,10 +43,6 @@
     for c in range(per):
         for i in (0, 1):
             loads_in[i * per + c].start()
-    for c in range(per):
-        for i in (2, 3):
-            loads_in[i * per + c].start()
-
     barrier = pltpu.get_barrier_semaphore()
     for k in range(1, nr):
         pl.semaphore_signal(barrier, inc=1, device_id={"sx": lax.rem(r + k, nr)}, device_id_type=MESH)
@@ -79,13 +75,32 @@
 
     EAST, SOUTH, NORTH, WEST = 0, per, 2 * per, 3 * per
 
-    def halo(k, slot, where_to):
+    def source_of(slot):
+        if slot == FROM_LEFT:
+            return per - 1
+        if slot == FROM_RIGHT:
+            return 0
+        return slot - (FROM_UP if slot < FROM_DOWN else FROM_DOWN)
+
+    def neighbour(src, dst, ssem, rsem, where_to):
         axis, shift = where_to
         index = (r if axis == "sx" else s) + shift
         return pltpu.make_async_remote_copy(
-            src_ref=snd.at[k, slot], dst_ref=rcv.at[k, slot],
-            send_sem=h_send.at[k, slot], recv_sem=h_recv.at[k, slot],
+            src_ref=src, dst_ref=dst, send_sem=ssem, recv_sem=rsem,
             device_id={axis: index}, device_id_type=MESH,
+        )
+
+    def halo(k, slot, where_to):
+        return neighbour(
+            snd.at[k, slot], rcv.at[k, slot], h_send.at[k, slot], h_recv.at[k, slot], where_to
+        )
+
+    def coupling_copy(slot, where_to):
+        return neighbour(cpad.at[source_of(slot)], ncp.at[slot], c_send.at[slot], c_recv.at[slot], where_to)
+
+    def solved_copy(k, slot, where_to):
+        return neighbour(
+            yo.at[k, source_of(slot)], yn.at[k, slot], n_send.at[k, slot], n_recv.at[k, slot], where_to
         )
 
     def route(slot):
@@ -96,6 +111,22 @@
         if slot < FROM_DOWN:
             return ("sx", 1), has_down, has_up
         return ("sx", -1), has_up, has_down
+
+    all_slots = range(2 + 2 * per)
+
+    def if_sending(slot, act):
+        to, can, _ = route(slot)
+
+        @pl.when(can)
+        def _():
+            act(to)
+
+    def if_getting(slot, act):
+        to, _, gets = route(slot)
+
+        @pl.when(gets)
+        def _():
+            act(to)
 
     def send(k, slot, value):
         snd[k, slot] = value.astype(BF16)
@@ -167,7 +198,10 @@
 
     cpad[...] = jnp.zeros(cpad.shape, BF16)
     for c in range(per):
-        cpad[c, 0:corners] = coup_ref[0, c]
+        cpad[c, 0:corners] = coup_ref[0, :, c, :]
+
+    for slot in all_slots:
+        if_sending(slot, lambda to, slot=slot: coupling_copy(slot, to).start())
 
     def combine(c, main, extra):
         flag = jnp.full((1, 1), wr_ref[0, c], jnp.int32).astype(F32).astype(BF16)
@@ -240,6 +274,8 @@
     for c in range(per):
         loads_in[c].wait()
         loads_in[per + c].wait()
+        loads_in[2 * per + c].start()
+        loads_in[3 * per + c].start()
         combine(c, am, aw)
     for slot, kind, c, there in [(FROM_LEFT, WEST, 0, has_left)] + [(FROM_UP + c, NORTH, c, has_up) for c in range(per)]:
         arrive(0, slot)
@@ -257,6 +293,12 @@
             mxc[k].wait_recv()
 
     def setup_end():
+        for c in range(per):
+            ct[c] = cpad[c].astype(F32).T.astype(BF16)
+        for slot in all_slots:
+            if_getting(slot, lambda to, slot=slot: coupling_copy(slot, to).wait_recv())
+            e = 0 if slot == FROM_LEFT else 2 if slot == FROM_RIGHT else 1 if slot < FROM_DOWN else 3
+            nct[slot] = ncp[slot].astype(F32).T[e * edge : (e + 1) * edge].astype(BF16)
         for k in range(nr - 1):
             cx[k].wait_recv()
         row_index = mz[:, 0:rows, :].reshape(ns * rows, 128)[:, 0:1]
@@ -313,9 +355,8 @@
         ]
         for copy in tcopies:
             copy.start()
-        half = len(blocks) // 2
-        for c, e in blocks[:half]:
-            loc[c, e * edge : (e + 1) * edge] = product(bm, c, e)
+        for c, e in blocks:
+            deliver(halo_round, c, e, product(bm, c, e), False)
         for copy in tcopies:
             copy.wait_recv()
         partial = jnp.dot(kmat[...], tp[number].reshape(nr * rows, 128), preferred_element_type=F32)
@@ -330,22 +371,35 @@
         ]
         for copy in ycopies:
             copy.start()
-        for c, e in blocks[half:]:
-            loc[c, e * edge : (e + 1) * edge] = product(bm, c, e)
         for copy in ycopies:
             copy.wait_recv()
         solved = yr[number, 0].astype(F32)
         for q in range(1, ns):
             solved = solved + yr[number, q].astype(F32)
         solved = solved.astype(BF16)
+        yo[number] = solved.reshape(per, SLOT, 128)
+        for slot in all_slots:
+            if_sending(slot, lambda to, slot=slot: solved_copy(number, slot, to).start())
         for c, e in blocks:
-            coarse = lax.dot_general(
-                cpad[c, :, e * edge : (e + 1) * edge] if (e * edge) % 128 == 0 and edge % 128 == 0 else cpad[c][:, e * edge : (e + 1) * edge],
-                solved[c * SLOT : (c + 1) * SLOT], (((0,), (0,)), ((), ())), preferred_element_type=F32,
+            loc[c, e * edge : (e + 1) * edge] = local_rows(c, e) + jnp.dot(
+                ct[c, e * edge : (e + 1) * edge], solved[c * SLOT : (c + 1) * SLOT], preferred_element_type=F32
             )
-            deliver(halo_round, c, e, local_rows(c, e) + coarse, False)
+
+        def across(slot):
+            if_getting(slot, lambda to: solved_copy(number, slot, to).wait_recv())
+            return jnp.dot(nct[slot], yn[number, slot], preferred_element_type=F32)
+
         for kind, c in everything:
-            value = jnp.where(mask_of(kind, c), gathered(halo_round, kind, c), 0.0)
+            value = gathered(halo_round, kind, c)
+            if kind == EAST and c == per - 1:
+                value = value - across(FROM_RIGHT)
+            elif kind == SOUTH:
+                value = value - across(FROM_DOWN + c)
+            elif kind == NORTH:
+                value = value + across(FROM_UP + c)
+            elif kind == WEST:
+                value = value + across(FROM_LEFT)
+            value = jnp.where(mask_of(kind, c), value, 0.0)
             put(kind, c, 0.5 * (ld[kind + c] - value))
         halo_round += 1
         for copy in tcopies + ycopies:
@@ -360,12 +414,21 @@
 
     for copy in cz + mzc + mxc + cx:
         copy.wait_send()
+    for slot in all_slots:
+        if_sending(slot, lambda to, slot=slot: coupling_copy(slot, to).wait_send())
+        for number in range(ITERS):
+            if_sending(slot, lambda to, slot=slot, number=number: solved_copy(number, slot, to).wait_send())
     down_right = [FROM_LEFT] + [FROM_UP + c for c in range(per)]
     up_left = [FROM_RIGHT] + [FROM_DOWN + c for c in range(per)]
     for k in range(halo_round + 1):
         slots = down_right if k == 0 else up_left if k == halo_round else down_right + up_left
         for slot in slots:
             left_behind(k, slot)
+
+
+def hand_over(mult_ref, prec_ref, mult_out, prec_out):
+    mult_out[...] = mult_ref[...]
+    prec_out[...] = prec_ref[...]
 
 
 def local(nr, ns, *args):
@@ -391,6 +454,9 @@
         pltpu.VMEM((3 * per + 1, edge, width), F32),
         pltpu.VMEM((3 * per + 1, edge, width), F32),
         pltpu.VMEM((per, SLOT, size), BF16),
+        pltpu.VMEM((slots, SLOT, size), BF16),
+        pltpu.VMEM((per, size, SLOT), BF16),
+        pltpu.VMEM((slots, edge, SLOT), BF16),
         pltpu.VMEM((meta_rows, 128), jnp.int32),
         pltpu.VMEM((ns, meta_rows, 128), jnp.int32),
         pltpu.VMEM((nr, meta_rows, 128), jnp.int32),
@@ -400,6 +466,8 @@
         pltpu.VMEM((ITERS, nr, rows, width), BF16),
         pltpu.VMEM((ITERS, ns, rows, width), BF16),
         pltpu.VMEM((ITERS, ns, rows, width), BF16),
+        pltpu.VMEM((ITERS, per, SLOT, width), BF16),
+        pltpu.VMEM((ITERS, slots, SLOT, width), BF16),
         dma((4 * per,)),
         dma((rounds, slots)), dma((rounds, slots)),
         dma((ns,)), dma((ns,)),
@@ -408,9 +476,12 @@
         dma((nr,)), dma((nr,)),
         dma((ITERS, nr)), dma((ITERS, nr)),
         dma((ITERS, ns)), dma((ITERS, ns)),
+        dma((slots,)), dma((slots,)),
+        dma((ITERS, slots)), dma((ITERS, slots)),
     ]
     out = jax.ShapeDtypeStruct(adjoint_loads.shape, F32)
-    return pl.pallas_call(
+    args = args[:5] + (jnp.transpose(coupling, (0, 2, 1, 3)),) + args[6:]
+    results = pl.pallas_call(
         functools.partial(kernel, nr, ns),
         out_shape=(out, out),
         in_specs=[vmem, hbm, hbm, hbm, hbm, vmem, vmem, smem, smem, smem],
@@ -420,6 +491,9 @@
             collective_id=0, has_side_effects=True, vmem_limit_bytes=60 * 1024 * 1024
         ),
     )(*args)
+    return pl.pallas_call(
+        hand_over, out_shape=(out, out), in_specs=[vmem, vmem], out_specs=(vmem, vmem)
+    )(*results)
 
 
 def solution(mesh):

time: 66.5 us -> 62.2 us (0.935)
  local copies, waits for them, and re-layouts: 5.29 us -> 0 us
  Pallas kernels: 60.3 us -> 61.4 us
    unnamed x3 -> x0, local copies, waits for them, and re-layouts: 5.29 us -> none
    pallas_call x0 -> x1, Pallas kernels: none -> 2.29 us  [local(): pl.pallas_call(hand_over, out_shape=(out, out), in_specs=[vmem, vmem], ou...]
    pallas_call x1, Pallas kernels: 60.3 us -> 59.1 us  [local(): pl.pallas_call(functools.partial(kernel, nr, ns), out_shape=(out, out), i...]
where the time goes in v2:
time: 62.2 us; the launch traced here: 62 us
  Pallas kernels  61.4 us (99%)
  between operations  0.64 us (1%)
    pallas_call x1, Pallas kernels, local(): pl.pallas_call(functools.partial(kernel, nr, ns), out_shape=(out, out), i...  59.1 us
    pallas_call x1, Pallas kernels, local(): pl.pallas_call(hand_over, out_shape=(out, out), in_specs=[vmem, vmem], ou...  2.29 us

profile of v2, /device:TPU:0, one launch (start us, length us, event | category | flops | bytes accessed | tf_op | source)
XLA Modules:
  0.0 62.0 jit_solution(5471382385480155607)
XLA Ops:
  0.6 59.1 %shard_map.113 = (f32[1,2,2,288,128]{4,3,2,1,0:T(8,128)}, f32[1,2,2,288,128]{4,3,2,1,0:T(8,128)}) custom-call(f32[1,2,2,288,128]{4,3,2,1,0:T(8,128)} %loads_ref.1, bf16[1,2,1152,1152]{3,2,1,0:T(8,128)(2,1)} %dual_t.1, bf16[1,2,1152,1152]{3,2,1,0:T(8,128)(2,1)} %dual_w.1, bf16[1,2,1152,1152]{3,2,1,0:T(8,128)(2,1)} %diri_t.1, ...), custom_call_target="tpu_custom_call" | custom-call | tf_op jit(solution)/shard_map/pallas_call | solution.py:484
  59.8 2.3 %shard_map.114 = (f32[1,2,2,288,128]{4,3,2,1,0:T(8,128)}, f32[1,2,2,288,128]{4,3,2,1,0:T(8,128)}) custom-call(f32[1,2,2,288,128]{4,3,2,1,0:T(8,128)} %get-tuple-element.4.mult_ref, f32[1,2,2,288,128]{4,3,2,1,0:T(8,128)} %get-tuple-element.5.prec_ref), custom_call_target="tpu_custom_call" | custom-call | tf_op jit(solution)/shard_map/pallas_call | solution.py:494

commit v3 on v2

--- a/solution.py
+++ b/solution.py
@@ -292,13 +292,15 @@
         for k in range(nr - 1):
             mxc[k].wait_recv()
 
-    def setup_end():
+    def setup_coupling():
         for c in range(per):
             ct[c] = cpad[c].astype(F32).T.astype(BF16)
         for slot in all_slots:
             if_getting(slot, lambda to, slot=slot: coupling_copy(slot, to).wait_recv())
             e = 0 if slot == FROM_LEFT else 2 if slot == FROM_RIGHT else 1 if slot < FROM_DOWN else 3
             nct[slot] = ncp[slot].astype(F32).T[e * edge : (e + 1) * edge].astype(BF16)
+
+    def setup_coarse():
         for k in range(nr - 1):
             cx[k].wait_recv()
         row_index = mz[:, 0:rows, :].reshape(ns * rows, 128)[:, 0:1]
@@ -329,7 +331,6 @@
                 loads_in[2 * per + c].wait()
                 loads_in[3 * per + c].wait()
                 combine(c, bm, bw)
-            setup_end()
         for kind, c in everything:
             value = jnp.where(mask_of(kind, c), 0.5 * gathered(halo_round, kind, c), 0.0)
             if number == 0:
@@ -356,7 +357,12 @@
         for copy in tcopies:
             copy.start()
         for c, e in blocks:
-            deliver(halo_round, c, e, product(bm, c, e), False)
+            value = product(bm, c, e)
+            loc[c, e * edge : (e + 1) * edge] = value
+            if slot_of(c, e) is not None:
+                snd[halo_round, slot_of(c, e)] = value.astype(BF16)
+        if number == 0:
+            setup_coarse()
         for copy in tcopies:
             copy.wait_recv()
         partial = jnp.dot(kmat[...], tp[number].reshape(nr * rows, 128), preferred_element_type=F32)
@@ -371,6 +377,12 @@
         ]
         for copy in ycopies:
             copy.start()
+        for c, e in blocks:
+            slot = slot_of(c, e)
+            if slot is not None:
+                if_sending(slot, lambda to, slot=slot: halo(halo_round, slot, to).start())
+        if number == 0:
+            setup_coupling()
         for copy in ycopies:
             copy.wait_recv()
         solved = yr[number, 0].astype(F32)

time: 62.2 us -> 58.3 us (0.937)
  Pallas kernels: 61.4 us -> 57.5 us
    pallas_call x1, Pallas kernels: 59.1 us -> 55.2 us  [local(): pl.pallas_call(functools.partial(kernel, nr, ns), out_shape=(out, out), i...]
where the time goes in v3:
time: 58.3 us; the launch traced here: 58.1 us
  Pallas kernels  57.5 us (99%)
  between operations  0.64 us (1%)
    pallas_call x1, Pallas kernels, local(): pl.pallas_call(functools.partial(kernel, nr, ns), out_shape=(out, out), i...  55.2 us
    pallas_call x1, Pallas kernels, local(): pl.pallas_call(hand_over, out_shape=(out, out), in_specs=[vmem, vmem], ou...  2.29 us

profile of v3, /device:TPU:0, one launch (start us, length us, event | category | flops | bytes accessed | tf_op | source)
XLA Modules:
  0.0 58.1 jit_solution(16952431647667925756)
XLA Ops:
  0.6 55.2 %shard_map.113 = (f32[1,2,2,288,128]{4,3,2,1,0:T(8,128)}, f32[1,2,2,288,128]{4,3,2,1,0:T(8,128)}) custom-call(f32[1,2,2,288,128]{4,3,2,1,0:T(8,128)} %loads_ref.1, bf16[1,2,1152,1152]{3,2,1,0:T(8,128)(2,1)} %dual_t.1, bf16[1,2,1152,1152]{3,2,1,0:T(8,128)(2,1)} %dual_w.1, bf16[1,2,1152,1152]{3,2,1,0:T(8,128)(2,1)} %diri_t.1, ...), custom_call_target="tpu_custom_call" | custom-call | tf_op jit(solution)/shard_map/pallas_call | solution.py:496
  55.8 2.3 %shard_map.114 = (f32[1,2,2,288,128]{4,3,2,1,0:T(8,128)}, f32[1,2,2,288,128]{4,3,2,1,0:T(8,128)}) custom-call(f32[1,2,2,288,128]{4,3,2,1,0:T(8,128)} %get-tuple-element.4.mult_ref, f32[1,2,2,288,128]{4,3,2,1,0:T(8,128)} %get-tuple-element.5.prec_ref), custom_call_target="tpu_custom_call" | custom-call | tf_op jit(solution)/shard_map/pallas_call | solution.py:506

commit v4 on v3

--- a/solution.py
+++ b/solution.py
@@ -361,6 +361,8 @@
             loc[c, e * edge : (e + 1) * edge] = value
             if slot_of(c, e) is not None:
                 snd[halo_round, slot_of(c, e)] = value.astype(BF16)
+                if e in (1, 3):
+                    if_sending(slot_of(c, e), lambda to, slot=slot_of(c, e): halo(halo_round, slot, to).start())
         if number == 0:
             setup_coarse()
         for copy in tcopies:
@@ -379,7 +381,7 @@
             copy.start()
         for c, e in blocks:
             slot = slot_of(c, e)
-            if slot is not None:
+            if slot is not None and e in (0, 2):
                 if_sending(slot, lambda to, slot=slot: halo(halo_round, slot, to).start())
         if number == 0:
             setup_coupling()

time: 58.3 us -> 59.3 us (1.017)
  Pallas kernels: 57.5 us -> 58.5 us
    pallas_call x1, Pallas kernels: 55.2 us -> 56.3 us  [local(): pl.pallas_call(functools.partial(kernel, nr, ns), out_shape=(out, out), i...]
where the time goes in v4:
time: 59.3 us; the launch traced here: 59.2 us
  Pallas kernels  58.5 us (99%)
  between operations  0.64 us (1%)
    pallas_call x1, Pallas kernels, local(): pl.pallas_call(functools.partial(kernel, nr, ns), out_shape=(out, out), i...  56.3 us
    pallas_call x1, Pallas kernels, local(): pl.pallas_call(hand_over, out_shape=(out, out), in_specs=[vmem, vmem], ou...  2.29 us

profile of v4, /device:TPU:0, one launch (start us, length us, event | category | flops | bytes accessed | tf_op | source)
XLA Modules:
  0.0 59.2 jit_solution(1945457102192780981)
XLA Ops:
  0.6 56.3 %shard_map.113 = (f32[1,2,2,288,128]{4,3,2,1,0:T(8,128)}, f32[1,2,2,288,128]{4,3,2,1,0:T(8,128)}) custom-call(f32[1,2,2,288,128]{4,3,2,1,0:T(8,128)} %loads_ref.1, bf16[1,2,1152,1152]{3,2,1,0:T(8,128)(2,1)} %dual_t.1, bf16[1,2,1152,1152]{3,2,1,0:T(8,128)(2,1)} %dual_w.1, bf16[1,2,1152,1152]{3,2,1,0:T(8,128)(2,1)} %diri_t.1, ...), custom_call_target="tpu_custom_call" | custom-call | tf_op jit(solution)/shard_map/pallas_call | solution.py:498
  56.9 2.3 %shard_map.114 = (f32[1,2,2,288,128]{4,3,2,1,0:T(8,128)}, f32[1,2,2,288,128]{4,3,2,1,0:T(8,128)}) custom-call(f32[1,2,2,288,128]{4,3,2,1,0:T(8,128)} %get-tuple-element.4.mult_ref, f32[1,2,2,288,128]{4,3,2,1,0:T(8,128)} %get-tuple-element.5.prec_ref), custom_call_target="tpu_custom_call" | custom-call | tf_op jit(solution)/shard_map/pallas_call | solution.py:508
